TPU v7x, 256 devices: a whole 4x4x8 slice. The times are simulated.
256 devices in a mesh: row: 16 (over z_hi, y), col: 16 (over z_lo, x, core).
Axes of the slice: x: 4, y: 4, z: 8 (z_hi: 4, z_lo: 2; z = z_hi * 2 + z_lo), core: 2. Of those that a mesh axis runs over, the one named last changes fastest.
Arguments:
- spectra: bfloat16 [4096, 128], P(('row', 'col')), may hold values from -6 to 6
- residual: bfloat16 [768, 128, 128, 128], P(('row', 'col')), may hold values from -1.5 to 1.5
- slot_tile: int32 [768], P(('row', 'col')), may hold values from -1 to 527, as said below
- tile_blocks: int32 [528, 2], replicated, may hold values from 0 to 31, as said below
Outputs:
- spectra_grad: float32 [4096, 128], P(('row', 'col'))
Inputs may be any that keep to these rules, and one draw needn't show every extreme that they name: `slot_tile`: every tile number appears in exactly one slot and all other slots hold -1. A tile with row block p and column block q sits on the device at mesh position (p mod 16, q mod 16), that is device number (p mod 16) * 16 + q mod 16 in the order of row+col. `tile_blocks`: row t holds the row block and the column block of tile t, the row block no larger than the column block; every such pair of blocks is exactly one tile.
All inputs are finite; a program needn't handle non-finite values.
Results may differ from a plain program's by a relative error of at most 0.004.
Values may be sent and summed in bfloat16 or wider, within the bound.
No kernel may reach another device: no remote copies, remote signals or barrier semaphores. Data moves between devices by JAX's collectives and lax.ppermute only.
A program may use at most 128 MiB of HBM per device.

v0:
```python
import math

import jax
import jax.numpy as jnp
from jax import lax
from jax.sharding import PartitionSpec as P


def dft_table(lag_count, freq_count):
    lag_index = jnp.arange(lag_count, dtype=jnp.int32) - lag_count // 2
    freq_index = jnp.arange(freq_count, dtype=jnp.int32)
    phase_steps = lag_index[:, None] * freq_index[None, :] % lag_count
    angles = phase_steps.astype(jnp.float32) * (2.0 * math.pi / lag_count)
    cosine = jnp.cos(angles) / lag_count
    sine = -jnp.sin(angles) / lag_count
    return jnp.concatenate([cosine, sine], axis=1).astype(jnp.bfloat16)


def pair_terms(spectral, row_spec, col_spec, freq_count):
    real_part = spectral[:, :, :freq_count]
    imag_part = spectral[:, :, freq_count:]
    row_re = row_spec[:, :freq_count].astype(jnp.float32)
    row_im = row_spec[:, freq_count:].astype(jnp.float32)
    col_re = col_spec[:, :freq_count].astype(jnp.float32)
    col_im = col_spec[:, freq_count:].astype(jnp.float32)
    row_gain_re = jnp.sum(real_part * col_re[None] - imag_part * col_im[None], axis=1)
    row_gain_im = jnp.sum(real_part * col_im[None] + imag_part * col_re[None], axis=1)
    col_gain_re = jnp.sum(real_part * row_re[:, None] + imag_part * row_im[:, None], axis=0)
    col_gain_im = jnp.sum(real_part * row_im[:, None] - imag_part * row_re[:, None], axis=0)
    row_gain = jnp.concatenate([row_gain_re, row_gain_im], axis=1)
    col_gain = jnp.concatenate([col_gain_re, col_gain_im], axis=1)
    return (row_gain, col_gain)


def block_major(flat, row_count, col_count, block_count, tile_size):
    per_row = block_count // row_count
    piece = tile_size // col_count
    grid = flat.reshape(row_count, col_count, per_row, piece, flat.shape[1])
    return jnp.transpose(grid, (2, 0, 1, 3, 4)).reshape(block_count, tile_size, flat.shape[1])


def station_major(blocks, row_count, col_count, block_count, tile_size):
    per_row = block_count // row_count
    piece = tile_size // col_count
    grid = blocks.reshape(per_row, row_count, col_count, piece, blocks.shape[2])
    return jnp.transpose(grid, (1, 2, 0, 3, 4)).reshape(block_count * tile_size, blocks.shape[2])


def add_block(gradient, contrib, index):
    current = lax.dynamic_index_in_dim(gradient, index, 0, keepdims=True)
    return lax.dynamic_update_index_in_dim(gradient, current + contrib[None], index, 0)


def on_device(spectra, residual, slot_tile, tile_blocks):
    slot_count, tile_size, _, lag_count = residual.shape
    freq_count = spectra.shape[1] // 2
    width = 2 * freq_count
    row_count = lax.axis_size("row")
    col_count = lax.axis_size("col")
    block_count = 2 * min(row_count, col_count)
    dft = dft_table(lag_count, freq_count)
    tile_total = tile_blocks.shape[0]
    matches = (slot_tile[:, None] == jnp.arange(tile_total, dtype=jnp.int32)[None, :]).astype(
        jnp.int32
    )
    chosen = jnp.sum(matches[:, :, None] * tile_blocks[None, :, :], axis=1)
    filled = slot_tile >= 0
    station_ids = jnp.arange(tile_size, dtype=jnp.int32)
    upper = station_ids[:, None] < station_ids[None, :]
    gathered = lax.all_gather(spectra, ("row", "col"), axis=0, tiled=True)
    row_source = block_major(gathered, row_count, col_count, block_count, tile_size)
    row_div = 1
    col_div = 1
    row_grad = jnp.zeros((row_source.shape[0], tile_size, width), jnp.float32)
    col_grad = jnp.zeros((row_source.shape[0], tile_size, width), jnp.float32)
    for slot_index in range(slot_count):
        row_block = chosen[slot_index, 0]
        col_block = chosen[slot_index, 1]
        pair_mask = (jnp.where(row_block == col_block, upper, True) & filled[slot_index]).astype(
            jnp.float32
        )
        tile_data = residual[slot_index]
        row_index = row_block // row_div
        col_index = col_block // col_div
        row_spec = lax.dynamic_index_in_dim(row_source, row_index, 0, keepdims=False)
        col_spec = lax.dynamic_index_in_dim(row_source, col_index, 0, keepdims=False)
        spectral = jnp.dot(
            tile_data.reshape(tile_size * tile_size, lag_count),
            dft,
            preferred_element_type=jnp.float32,
        )
        spectral = spectral.reshape(tile_size, tile_size, width) * pair_mask[:, :, None]
        row_gain, col_gain = pair_terms(spectral, row_spec, col_spec, freq_count)
        row_grad = add_block(row_grad, row_gain, row_index)
        col_grad = add_block(col_grad, col_gain, col_index)
    gradient = station_major(row_grad + col_grad, row_count, col_count, block_count, tile_size)
    return lax.psum_scatter(gradient, ("row", "col"), scatter_dimension=0, tiled=True)


def solution(mesh):
    return jax.shard_map(
        on_device,
        mesh=mesh,
        in_specs=(
            P(("row", "col"), None),
            P(("row", "col"), None, None, None),
            P(("row", "col")),
            P(),
        ),
        out_specs=P(("row", "col"), None),
        check_vma=False,
    )
```

profile of v0, /device:TPU:1, one launch (start us, length us, event | category | flops | bytes accessed | tf_op | source)
XLA Modules:
  0.0 1709.8 jit_solution(4478842264416761182)
XLA Ops:
  6.5 0.7 all-gather.2.cloned.1.call-update
  7.3 0.7 fusion.25
  8.0 0.7 broadcast_compare_fusion
  8.7 0.8 multiply_reduce_fusion
  10.1 0.7 fusion.37
  11.0 8.2 fusion.29
  19.1 4.5 convolution_bitcast_fusion.2
  23.6 4.5 convolution_bitcast_fusion.1
  28.1 4.5 convolution_bitcast_fusion
  35.4 0.7 fusion.16
  44.6 8.2 copy.80
  52.9 8.2 copy.81
  61.1 4.7 copy.82
  70.0 8.9 bitcast_multiply_fusion.2
  78.9 4.2 bitcast_multiply_fusion.1
  83.1 4.2 bitcast_multiply_fusion
  87.3 309.4 %all-gather.2.cloned.1.call-done = bf16[4096,128]{1,0:T(8,128)(2,1)} async-done(((bf16[16,128]{1,0:T(8,128)(2,1)}), bf16[4096,128]{1,0:T(8,128)(2,1)}) %all-gather.2.cloned.1.call-update) | async-done | bytes 1048592 | tf_op jit(solution)/shard_map/all_gather | solution.py:70
  396.7 1.5 copy.53
  399.9 8.5 add_reduce_fusion.2
  408.7 5.2 add_reduce_fusion.1
  414.0 5.2 add_reduce_fusion
  419.7 1.9 copy.66
  421.6 3.1 copy.67
  424.7 1278.2 %reduce-scatter.2.cloned.1.call-done = f32[16,128]{1,0:T(8,128)} async-done(((f32[4096,128]{1,0:T(8,128)}), f32[16,128]{1,0:T(8,128)}) %reduce-scatter.2.cloned.1.call-update) | async-done | bytes 8208 | tf_op jit(solution)/shard_map/reduce_scatter | solution.py:97
  (64 shorter events, 4.3 us)
Async XLA Ops:
  6.5 390.2 %all-gather.2.cloned.1.call-start = ((), (), s32[]{:S(2)}) async-start(), calls=%async_computation.1 | async-start | bytes 1052672 | tf_op jit(solution)/shard_map/all_gather | solution.py:70
  7.3 1695.7 %reduce-scatter.2.cloned.1.call-start = ((), (), s32[]{:S(2)}) async-start(), calls=%async_computation.2 | async-start | bytes 2105344 | tf_op jit(solution)/shard_map/reduce_scatter | solution.py:97
  44.6 16.4 slice-start.4
  52.9 8.2 slice-start.5
  70.0 8.9 copy-start.1
  70.0 13.1 slice-start.2
  78.9 4.2 slice-start.3
  399.9 8.8 copy-start
  399.9 14.0 slice-start
  408.4 5.5 slice-start.1
Sparse Core Ops, SparseCore 0:
  9.1 387.5 all-gather.1
  424.8 1278.0 reduce-scatter.1
where the time goes:
time: 1710 us
  waiting for transfers between devices  1590 us (93%)
  other arithmetic  40.8 us (2%)
  local copies, waits for them, and re-layouts  38.9 us (2%)
  between operations  28.2 us (2%)
    reduce_scatter x1, waiting for transfers between devices, on_device(): lax.psum_scatter(gradient, ('row', 'col'), scatter_dimension=0, tiled=True)  1280 us
    all_gather x1, waiting for transfers between devices, on_device(): gathered = lax.all_gather(spectra, ('row', 'col'), axis=0, tiled=True)  309 us
  transfers between devices with their start and end apart: 2, of which 2 were waited for; matrix products, arithmetic and copies ran while one was open for 4% of the time, Pallas kernels for 0%

commit v1 on v0

v1 whole, which is shorter than its diff:
```python
import functools
import math

import jax
import jax.numpy as jnp
import ml_dtypes
import numpy as np
from jax import lax
from jax.experimental import pallas as pl
from jax.experimental.pallas import tpu as pltpu
from jax.sharding import PartitionSpec as P

F = 64
L = 128
BS = 128
SLOTS = 3
NB = 32
CHUNK = 64
N_CHUNK = BS // CHUNK
UNROLL = 16


def dft_pair():
    lag = np.arange(L, dtype=np.int64) - L // 2
    freq = np.arange(F, dtype=np.int64)
    steps = (lag[:, None] * freq[None, :]) % L
    angles = steps.astype(np.float32) * np.float32(2.0 * math.pi / L)
    table = np.concatenate([np.cos(angles) / L, -np.sin(angles) / L], axis=1)
    zero = np.zeros((L, 2 * F))
    return np.block([[table, zero], [zero, table]]).astype(ml_dtypes.bfloat16)


def spec_pair(spec_ref, upper, filled):
    both = spec_ref[...].astype(jnp.float32)
    block = jnp.where(upper == 1, both[:, BS // 16 :, :], both[:, : BS // 16, :])
    block = block.reshape(BS, 2 * F) * filled
    return block, pltpu.roll(block, F, axis=1)


def load_all(res_hbm, buf, sems):
    for s in range(SLOTS):
        for c in range(N_CHUNK):
            pltpu.make_async_copy(
                res_hbm.at[s, pl.ds(c * CHUNK, CHUNK)],
                buf.at[s, pl.ds(c * CHUNK, CHUNK)],
                sems.at[s, c],
            ).start()


def wait_chunk(res_hbm, buf, sems, s, c):
    pltpu.make_async_copy(
        res_hbm.at[s, pl.ds(c * CHUNK, CHUNK)], buf.at[s, pl.ds(c * CHUNK, CHUNK)], sems.at[s, c]
    ).wait()


def mask_chunk(buf, s, first):
    def one(n, carry):
        i = first + n
        rows = lax.broadcasted_iota(jnp.int32, (BS, L), 0)
        keep = jnp.where(rows > i, 1.0, 0.0).astype(jnp.bfloat16)
        buf[s, i] = buf[s, i] * keep
        return carry

    lax.fori_loop(0, CHUNK, one, 0)


def decode(enc_ref, s):
    code = enc_ref[s]
    filled = jnp.where(code > 0, 1.0, 0.0).astype(jnp.float32)
    tile = jnp.maximum(code - 1, 0)
    p = tile // NB
    q = tile - p * NB
    return p, q, filled


def col_kernel(enc_ref, spec_ref, dft_ref, res_hbm, out_ref, buf, one_ref, two_ref, acc_ref, sems):
    load_all(res_hbm, buf, sems)
    acc_ref[...] = jnp.zeros_like(acc_ref)

    def slot(s, carry):
        p, q, filled = decode(enc_ref, s)
        one, two = spec_pair(spec_ref, p // 16, filled)
        one_ref[...] = one
        two_ref[...] = two
        total = (jnp.zeros((BS, 2 * F), jnp.float32),) * 2
        for c in range(N_CHUNK):
            wait_chunk(res_hbm, buf, sems, s, c)

            @pl.when(p == q)
            def _():
                mask_chunk(buf, s, c * CHUNK)

            def step(n, total):
                t1, t2 = total
                base = c * CHUNK + n * UNROLL
                for u in range(0, UNROLL, 2):
                    lhs = jnp.concatenate([buf[s, base + u], buf[s, base + u + 1]], axis=1)
                    g = jnp.dot(lhs, dft_ref[...], preferred_element_type=jnp.float32)
                    for h in range(2):
                        gh = g[:, h * L : (h + 1) * L]
                        t1 = t1 + gh * one_ref[pl.ds(base + u + h, 1), :]
                        t2 = t2 + gh * two_ref[pl.ds(base + u + h, 1), :]
                return t1, t2

            total = lax.fori_loop(0, CHUNK // UNROLL, step, total)
        t1, t2 = total
        lane = lax.broadcasted_iota(jnp.int32, (BS, 2 * F), 1)
        gain = jnp.where(lane < F, t1 + pltpu.roll(t1, F, axis=1), pltpu.roll(t2, F, axis=1) - t2)
        gain = gain.reshape(16, BS // 16, 2 * F)
        for h in range(2):
            rows = pl.ds(h * 8, 8)

            @pl.when(q // 16 == h)
            def _():
                acc_ref[:, rows, :] = acc_ref[:, rows, :] + gain

        return carry

    lax.fori_loop(0, SLOTS, slot, 0)
    out_ref[...] = acc_ref[...].astype(out_ref.dtype)


def row_kernel(enc_ref, spec_ref, dft_ref, res_hbm, out_ref, buf, one_ref, two_ref, part1, part2, sems):
    load_all(res_hbm, buf, sems)
    out_ref[...] = jnp.zeros_like(out_ref)

    def slot(s, carry):
        p, q, filled = decode(enc_ref, s)
        one, two = spec_pair(spec_ref, q // 16, filled)
        one_ref[...] = one
        two_ref[...] = two
        for c in range(N_CHUNK):
            wait_chunk(res_hbm, buf, sems, s, c)

            @pl.when(p == q)
            def _():
                mask_chunk(buf, s, c * CHUNK)

            def step(n, carry):
                base = c * CHUNK + n * UNROLL
                for u in range(0, UNROLL, 2):
                    lhs = jnp.concatenate([buf[s, base + u], buf[s, base + u + 1]], axis=1)
                    g = jnp.dot(lhs, dft_ref[...], preferred_element_type=jnp.float32)
                    for h in range(2):
                        gh = g[:, h * L : (h + 1) * L]
                        for ref, part in ((one_ref, part1), (two_ref, part2)):
                            prod = (gh * ref[...]).reshape(BS // 8, 8, 2 * F)
                            at = pl.multiple_of((base + u + h) * 8, 8)
                            part[pl.ds(at, 8), :] = jnp.sum(prod, axis=0)
                return carry

            lax.fori_loop(0, CHUNK // UNROLL, step, 0)
        t1 = jnp.zeros((BS, 2 * F), jnp.float32)
        t2 = jnp.zeros((BS, 2 * F), jnp.float32)
        for k in range(8):
            t1 = t1 + part1[pl.ds(k, BS, stride=8), :]
            t2 = t2 + part2[pl.ds(k, BS, stride=8), :]
        lane = lax.broadcasted_iota(jnp.int32, (BS, 2 * F), 1)
        gain = jnp.where(lane < F, t1 - pltpu.roll(t1, F, axis=1), pltpu.roll(t2, F, axis=1) + t2)
        gain = gain.reshape(16, BS // 16, 2 * F)
        for h in range(2):
            rows = pl.ds(h * 8, 8)

            @pl.when(p // 16 == h)
            def _():
                out_ref[:, rows, :] = out_ref[:, rows, :] + gain

        return carry

    lax.fori_loop(0, SLOTS, slot, 0)


def call(kernel, name, out_dtype, scratch, enc, spec, dft, residual):
    vmem = pl.BlockSpec(memory_space=pltpu.VMEM)
    return pl.pallas_call(
        kernel,
        name=name,
        out_shape=jax.ShapeDtypeStruct((16, 16, 2 * F), out_dtype),
        in_specs=[
            pl.BlockSpec(memory_space=pltpu.SMEM),
            vmem,
            vmem,
            pl.BlockSpec(memory_space=pl.ANY),
        ],
        out_specs=vmem,
        scratch_shapes=[
            pltpu.VMEM((SLOTS, BS, BS, L), jnp.bfloat16),
            pltpu.VMEM((BS, 2 * F), jnp.float32),
            pltpu.VMEM((BS, 2 * F), jnp.float32),
            *scratch,
            pltpu.SemaphoreType.DMA((SLOTS, N_CHUNK)),
        ],
        compiler_params=pltpu.CompilerParams(vmem_limit_bytes=24 << 20),
        cost_estimate=pl.CostEstimate(
            flops=SLOTS * BS * BS * L * 2 * F * 2, bytes_accessed=residual.size * 2, transcendentals=0
        ),
    )(enc, spec, dft, residual)


def on_device(spectra, residual, slot_tile, tile_blocks):
    tiles = jnp.arange(tile_blocks.shape[0], dtype=jnp.int32)
    code = tile_blocks[:, 0] * NB + tile_blocks[:, 1] + 1
    enc = jnp.sum(jnp.where(slot_tile[:, None] == tiles[None, :], code[None, :], 0), axis=1)
    dft = jnp.asarray(dft_pair())
    swap = [(a * 16 + b, b * 16 + a) for a in range(16) for b in range(16)]
    spread = jnp.broadcast_to(spectra[None], (16, 16, 2 * F))
    row_spec = lax.all_to_all(spread, "col", 0, 0)
    col_spec = lax.ppermute(row_spec, ("row", "col"), swap)
    acc = pltpu.VMEM((16, 16, 2 * F), jnp.float32)
    part = pltpu.VMEM((BS * 8, 2 * F), jnp.float32)
    col_gain = call(col_kernel, "col_gain", jnp.bfloat16, [acc], enc, row_spec, dft, residual)
    moved = lax.ppermute(col_gain, ("row", "col"), swap)
    row_gain = call(row_kernel, "row_gain", jnp.float32, [part, part], enc, col_spec, dft, residual)
    total = (row_gain + moved.astype(jnp.float32)).astype(jnp.bfloat16)
    pieces = lax.all_to_all(total, "col", 0, 0)
    return jnp.sum(pieces.astype(jnp.float32), axis=0)


def solution(mesh):
    return jax.shard_map(
        on_device,
        mesh=mesh,
        in_specs=(
            P(("row", "col"), None),
            P(("row", "col"), None, None, None),
            P(("row", "col")),
            P(),
        ),
        out_specs=P(("row", "col"), None),
        check_vma=False,
    )
```

time: 1710 us -> 68 us (0.04)
  waiting for transfers between devices: 1590 us -> 4.2 us
  other arithmetic: 40.8 us -> 2.26 us
  local copies, waits for them, and re-layouts: 38.9 us -> 6.83 us
  between operations: 28.2 us -> 0.09 us
  Pallas kernels: 0 us -> 19.6 us
  starting transfers between devices: 0.04 us -> 17.4 us
  blocking collectives: 0 us -> 17.2 us
    reduce_scatter x1 -> x0, waiting for transfers between devices: 1280 us -> none  [on_device(): lax.psum_scatter(gradient, ('row', 'col'), scatter_dimension=0, tiled=True)]
    all_gather x1 -> x0, waiting for transfers between devices: 309 us -> none  [on_device(): gathered = lax.all_gather(spectra, ('row', 'col'), axis=0, tiled=True)]
    pallas_call x0 -> x2, Pallas kernels: none -> 19.6 us  [call(): pl.pallas_call(kernel, name=name, out_shape=jax.ShapeDtypeStruct((16, 16,...]
    reduce_sum x4 -> x2, other arithmetic: 19.7 us -> 1.46 us  [the longest x1 0.84 us: on_device(): jnp.sum(jnp.where(slot_tile[:, None] == tiles[None, :], code[None, :], 0)...]
    mul x3 -> x0, other arithmetic: 17.2 us -> none  [on_device(): spectral.reshape(tile_size, tile_size, width) * pair_mask[:, :, None]]
    all_to_all x0 -> x1, blocking collectives: none -> 17.2 us  [on_device(): pieces = lax.all_to_all(total, 'col', 0, 0)]
  transfers between devices with their start and end apart: 2 -> 3, of which waited for: 2 -> 1; matrix products, arithmetic and copies ran while one was open for 4% -> 2% of each run, Pallas kernels for 0% -> 29%
where the time goes in v1:
time: 68 us; the launch traced here: 67.7 us
  Pallas kernels  19.6 us (29%)
  starting transfers between devices  17.4 us (26%)
  blocking collectives  17.2 us (25%)
  local copies, waits for them, and re-layouts  6.83 us (10%)
  waiting for transfers between devices  4.2 us (6%)
  other arithmetic  2.26 us (3%)
    pallas_call x2, Pallas kernels, call(): pl.pallas_call(kernel, name=name, out_shape=jax.ShapeDtypeStruct((16, 16,...  19.6 us
    all_to_all x1, blocking collectives, on_device(): pieces = lax.all_to_all(total, 'col', 0, 0)  17.2 us
    all_to_all x1, starting transfers between devices, on_device(): row_spec = lax.all_to_all(spread, 'col', 0, 0)  7.16 us
    ppermute x1, starting transfers between devices, on_device(): moved = lax.ppermute(col_gain, ('row', 'col'), swap)  6.75 us
    unnamed x8, local copies, waits for them, and re-layouts  5.48 us
    all_to_all x1, waiting for transfers between devices, on_device(): row_spec = lax.all_to_all(spread, 'col', 0, 0)  4.2 us
    ppermute x1, starting transfers between devices, on_device(): col_spec = lax.ppermute(row_spec, ('row', 'col'), swap)  3.52 us
  transfers between devices with their start and end apart: 3, of which 1 were waited for; matrix products, arithmetic and copies ran while one was open for 2% of the time, Pallas kernels for 29%

profile of v1, /device:TPU:1, one launch (start us, length us, event | category | flops | bytes accessed | tf_op | source)
XLA Modules:
  0.0 67.7 jit_solution(7189528303347352267)
XLA Ops:
  0.0 0.0 copy-start.3
  0.0 1.3 %broadcast_in_dim.23 = bf16[16,16,128]{2,1,0:T(8,128)(2,1)} broadcast(bf16[16,128]{1,0:T(8,128)(2,1)} %param.5), dimensions={1,2} | broadcast | bytes 69632 | tf_op jit(solution)/shard_map/broadcast_in_dim | solution.py:206
  1.4 7.2 %all-to-all-start = ((bf16[16,16,128]{2,1,0:T(8,128)(2,1)}), bf16[16,16,128]{2,1,0:T(8,128)(2,1)S(1)}, u32[]{:S(2)}, u32[]{:S(2)}) async-start(bf16[16,16,128]{2,1,0:T(8,128)(2,1)} %broadcast_in_dim.23), calls=%async_computation | async-start | bytes 131072 | tf_op jit(solution)/shard_map/all_to_all | solution.py:207
  8.5 0.8 %add_reduce_fusion = s32[528]{0:T(1024)S(1)} fusion(s32[528,2]{0,1:T(2,128)} %param.8), kind=kLoop, calls=%fused_computation.4 | loop fusion | flops 1584 | bytes 6336 | tf_op jit(solution)/shard_map/add | solution.py:202
  9.3 0.8 %select_reduce_fusion.enc_ref = s32[3]{0:T(128)S(1)} fusion(s32[528]{0:T(1024)S(1)} %add_reduce_fusion, s32[3]{0:T(128)} %param.7), kind=kLoop, calls=%fused_computation.2 | loop fusion | flops 4749 | bytes 2136 | tf_op jit(solution)/shard_map/reduce_sum | solution.py:203
  10.1 4.2 %all-to-all-done.spec_ref = bf16[16,16,128]{2,1,0:T(8,128)(2,1)S(1)} async-done(((bf16[16,16,128]{2,1,0:T(8,128)(2,1)}), bf16[16,16,128]{2,1,0:T(8,128)(2,1)S(1)}, u32[]{:S(2)}, u32[]{:S(2)}) %all-to-all-start) | async-done | bytes 65568 | tf_op jit(solution)/shard_map/all_to_all | solution.py:207
  14.3 3.5 %collective-permute-start = (bf16[16,16,128]{2,1,0:T(8,128)(2,1)S(1)}, bf16[16,16,128]{2,1,0:T(8,128)(2,1)S(1)}, u32[]{:S(2)}, u32[]{:S(2)}) collective-permute-start(bf16[16,16,128]{2,1,0:T(8,128)(2,1)S(1)} %all-to-all-done.spec_ref), channel_id=1, source_target_pairs={{0,0},{1,16},{2,32},{3,48},{4,64},{5,80},{6,96},{7,112},{8,128},{9... | collective-permute-start | bytes 196616 | tf_op jit(solution)/shard_map/ppermute | solution.py:208
  17.9 0.0 copy-start
  17.9 4.6 %copy-done = bf16[3,128,128,128]{3,2,1,0:T(8,128)(2,1)S(1)} copy-done((bf16[3,128,128,128]{3,2,1,0:T(8,128)(2,1)S(1)}, bf16[3,128,128,128]{3,2,1,0:T(8,128)(2,1)}, u32[]{:S(2)}) %copy-start) | copy-done | bytes 12582936
  22.4 0.0 copy-start.2
  22.4 0.9 %copy-done.2 = bf16[256,256]{1,0:T(8,128)(2,1)S(1)} copy-done((bf16[256,256]{1,0:T(8,128)(2,1)S(1)}, bf16[256,256]{1,0:T(8,128)(2,1)}, u32[]{:S(2)}) %copy-start.2) | copy-done | bytes 131096
  23.3 0.0 copy-start.1
  23.3 9.8 %col_gain.1 = bf16[16,16,128]{2,1,0:T(8,128)(2,1)S(1)} custom-call(s32[3]{0:T(128)S(1)} %select_reduce_fusion.enc_ref, bf16[16,16,128]{2,1,0:T(8,128)(2,1)S(1)} %all-to-all-done.spec_ref, bf16[256,256]{1,0:T(8,128)(2,1)S(1)} %copy-done.2, bf16[3,128,128,128]{3,2,1,0:T(8,128)(2,1)S(1)} %copy-done), custom_call_target="tpu_custom_call" | custom-call | flops 1610612736 | bytes 12582912 | tf_op jit(solution)/shard_map/col_gain/pallas_call | solution.py:175
  33.1 6.8 %collective-permute-start.1 = (bf16[16,16,128]{2,1,0:T(8,128)(2,1)S(1)}, bf16[16,16,128]{2,1,0:T(8,128)(2,1)S(1)}, u32[]{:S(2)}, u32[]{:S(2)}) collective-permute-start(bf16[16,16,128]{2,1,0:T(8,128)(2,1)S(1)} %col_gain.1), channel_id=1, source_target_pairs={{0,0},{1,16},{2,32},{3,48},{4,64},{5,80},{6,96},{7,112},{8,128},{9... | collective-permute-start | bytes 196616 | tf_op jit(solution)/shard_map/ppermute | solution.py:212
  39.9 0.0 collective-permute-done.spec_ref
  39.9 0.0 copy-done.3
  39.9 0.0 copy-done.1
  39.9 9.9 %row_gain.1 = f32[16,16,128]{2,1,0:T(8,128)S(1)} custom-call(s32[3]{0:T(128)S(1)} %select_reduce_fusion.enc_ref, bf16[16,16,128]{2,1,0:T(8,128)(2,1)S(1)} %collective-permute-done.spec_ref, bf16[256,256]{1,0:T(8,128)(2,1)S(1)} %copy-done.3, bf16[3,128,128,128]{3,2,1,0:T(8,128)(2,1)S(1)} %copy-done.1), custom_call_target="tpu_custom_call" | custom-call | flops 1610612736 | bytes 12582912 | tf_op jit(solution)/shard_map/row_gain/pallas_call | solution.py:175
  49.8 0.0 collective-permute-done.1
  49.8 17.2 %all_to_all.10 = bf16[16,16,128]{2,1,0:T(8,128)(2,1)S(1)} all-to-all(bf16[16,16,128]{2,1,0:T(8,128)(2,1)S(1)} %add_convert_fusion), channel_id=1, replica_groups=mesh['row'=16,'col'=16] {'col'}, dimensions={0} | all-to-all | bytes 131072 | tf_op jit(solution)/shard_map/all_to_all | solution.py:215
  67.0 0.6 convert_reduce_fusion
  (1 shorter events, 0.0 us)
Async XLA Ops:
  0.0 39.9 %copy-start.3 = (bf16[256,256]{1,0:T(8,128)(2,1)S(1)}, bf16[256,256]{1,0:T(8,128)(2,1)}, u32[]{:S(2)}) copy-start(bf16[256,256]{1,0:T(8,128)(2,1)} %constant.10.clone.dft_ref) | copy-start | bytes 393220
  1.4 13.0 %all-to-all-start = ((bf16[16,16,128]{2,1,0:T(8,128)(2,1)}), bf16[16,16,128]{2,1,0:T(8,128)(2,1)S(1)}, u32[]{:S(2)}, u32[]{:S(2)}) async-start(bf16[16,16,128]{2,1,0:T(8,128)(2,1)} %broadcast_in_dim.23), calls=%async_computation | async-start | bytes 131072 | tf_op jit(solution)/shard_map/all_to_all | solution.py:207
  14.3 25.5 %collective-permute-start = (bf16[16,16,128]{2,1,0:T(8,128)(2,1)S(1)}, bf16[16,16,128]{2,1,0:T(8,128)(2,1)S(1)}, u32[]{:S(2)}, u32[]{:S(2)}) collective-permute-start(bf16[16,16,128]{2,1,0:T(8,128)(2,1)S(1)} %all-to-all-done.spec_ref), channel_id=1, source_target_pairs={{0,0},{1,16},{2,32},{3,48},{4,64},{5,80},{6,96},{7,112},{8,128},{9... | collective-permute-start | bytes 196616 | tf_op jit(solution)/shard_map/ppermute | solution.py:208
  17.9 4.6 %copy-start = (bf16[3,128,128,128]{3,2,1,0:T(8,128)(2,1)S(1)}, bf16[3,128,128,128]{3,2,1,0:T(8,128)(2,1)}, u32[]{:S(2)}) copy-start(bf16[3,128,128,128]{3,2,1,0:T(8,128)(2,1)} %res_hbm.3) | copy-start | bytes 37748740
  22.4 0.9 %copy-start.2 = (bf16[256,256]{1,0:T(8,128)(2,1)S(1)}, bf16[256,256]{1,0:T(8,128)(2,1)}, u32[]{:S(2)}) copy-start(bf16[256,256]{1,0:T(8,128)(2,1)} %constant.10.clone.dft_ref) | copy-start | bytes 393220
  23.3 16.6 %copy-start.1 = (bf16[3,128,128,128]{3,2,1,0:T(8,128)(2,1)S(1)}, bf16[3,128,128,128]{3,2,1,0:T(8,128)(2,1)}, u32[]{:S(2)}) copy-start(bf16[3,128,128,128]{3,2,1,0:T(8,128)(2,1)} %res_hbm.3) | copy-start | bytes 37748740
  33.1 16.7 %collective-permute-start.1 = (bf16[16,16,128]{2,1,0:T(8,128)(2,1)S(1)}, bf16[16,16,128]{2,1,0:T(8,128)(2,1)S(1)}, u32[]{:S(2)}, u32[]{:S(2)}) collective-permute-start(bf16[16,16,128]{2,1,0:T(8,128)(2,1)S(1)} %col_gain.1), channel_id=1, source_target_pairs={{0,0},{1,16},{2,32},{3,48},{4,64},{5,80},{6,96},{7,112},{8,128},{9... | collective-permute-start | bytes 196616 | tf_op jit(solution)/shard_map/ppermute | solution.py:212

commit v2 on v1

v2 whole, which is shorter than its diff:
```python
import functools
import math

import jax
import jax.numpy as jnp
import ml_dtypes
import numpy as np
from jax import lax
from jax.experimental import pallas as pl
from jax.experimental.pallas import tpu as pltpu
from jax.sharding import PartitionSpec as P

F = 64
L = 128
BS = 128
SLOTS = 3
NB = 32
CHUNK = 64
PARTS = SLOTS * BS // CHUNK
PER = BS // CHUNK
ROW_UNROLL = 16
VMEM_COL = 12 << 20
VMEM_ROW = 8 << 20


def dft_pair():
    lag = np.arange(L, dtype=np.int64) - L // 2
    freq = np.arange(F, dtype=np.int64)
    steps = (lag[:, None] * freq[None, :]) % L
    angles = steps.astype(np.float32) * np.float32(2.0 * math.pi / L)
    table = np.concatenate([np.cos(angles) / L, -np.sin(angles) / L], axis=1)
    zero = np.zeros((L, 2 * F))
    return np.block([[table, zero], [zero, table]]).astype(ml_dtypes.bfloat16)


def spec_pair(spec_ref, upper, filled):
    both = spec_ref[...].astype(jnp.float32)
    block = jnp.where(upper == 1, both[:, BS // 16 :, :], both[:, : BS // 16, :])
    block = block.reshape(BS, 2 * F) * filled.astype(jnp.float32)
    return block, pltpu.roll(block, F, axis=1)


def add_gain(ref, gain, half):
    gain = gain.reshape(16, BS // 16, 2 * F)
    for h in range(2):
        rows = pl.ds(h * 8, 8)

        @pl.when(half == h)
        def _():
            ref[:, rows, :] = ref[:, rows, :] + gain


def chunk_copy(res_hbm, buf, sems, h, slot):
    return pltpu.make_async_copy(res_hbm.at[pl.ds(h * CHUNK, CHUNK)], buf.at[slot], sems.at[slot])


def mask_chunk(buf, slot, first):
    def one(n, carry):
        rows = lax.broadcasted_iota(jnp.int32, (BS, L), 0)
        keep = jnp.where(rows > first + n, 1.0, 0.0).astype(jnp.bfloat16)
        buf[slot, n] = buf[slot, n] * keep
        return carry

    lax.fori_loop(0, CHUNK, one, 0)


def col_kernel(
    slot_hbm, table_hbm, dft_hbm, res_hbm, spec_ref, out_ref, g_ref, meta_ref,
    buf, dft_ref, slot_ref, table_ref, one_ref, two_ref, acc_ref, sems,
):
    small = [
        pltpu.make_async_copy(src, dst, sems.at[2 + n])
        for n, (src, dst) in enumerate(((slot_hbm, slot_ref), (table_hbm, table_ref), (dft_hbm, dft_ref)))
    ]
    for copy in small:
        copy.start()
    chunk_copy(res_hbm, buf, sems, 0, 0).start()
    acc_ref[...] = jnp.zeros_like(acc_ref)
    for copy in small:
        copy.wait()
    for s in range(SLOTS):
        tile = slot_ref[s]
        safe = jnp.maximum(tile, 0)
        meta_ref[s] = table_ref[0, safe]
        meta_ref[SLOTS + s] = table_ref[1, safe]
        meta_ref[2 * SLOTS + s] = jnp.where(tile >= 0, 1, 0)

    def part(h, carry):
        s = h // PER
        first = (h - s * PER) * CHUNK
        slot = lax.rem(h, 2)
        p, q, filled = meta_ref[s], meta_ref[SLOTS + s], meta_ref[2 * SLOTS + s]

        @pl.when(h + 1 < PARTS)
        def _():
            chunk_copy(res_hbm, buf, sems, h + 1, 1 - slot).start()

        one, two = spec_pair(spec_ref, p // 16, filled)
        one_ref[...] = one
        two_ref[...] = two
        chunk_copy(res_hbm, buf, sems, h, slot).wait()

        @pl.when(p == q)
        def _():
            mask_chunk(buf, slot, first)

        t1 = jnp.zeros((BS, 2 * F), jnp.float32)
        t2 = jnp.zeros((BS, 2 * F), jnp.float32)
        for u in range(0, CHUNK, 2):
            lhs = jnp.concatenate([buf[slot, u], buf[slot, u + 1]], axis=1)
            g = jnp.dot(lhs, dft_ref[...], preferred_element_type=jnp.float32)
            for k in range(2):
                gk = g[:, k * L : (k + 1) * L]
                g_ref[h * CHUNK + u + k] = gk
                t1 = t1 + gk * one_ref[pl.ds(first + u + k, 1), :]
                t2 = t2 + gk * two_ref[pl.ds(first + u + k, 1), :]
        lane = lax.broadcasted_iota(jnp.int32, (BS, 2 * F), 1)
        gain = jnp.where(lane < F, t1 + pltpu.roll(t1, F, axis=1), pltpu.roll(t2, F, axis=1) - t2)
        add_gain(acc_ref, gain, q // 16)
        return carry

    lax.fori_loop(0, PARTS, part, 0)
    out_ref[...] = acc_ref[...].astype(out_ref.dtype)


def row_kernel(meta_ref, spec_ref, g_ref, out_ref, one_ref, two_ref, part1, part2):
    out_ref[...] = jnp.zeros_like(out_ref)

    def slot(s, carry):
        p, q, filled = meta_ref[s], meta_ref[SLOTS + s], meta_ref[2 * SLOTS + s]
        one, two = spec_pair(spec_ref, q // 16, filled)
        one_ref[...] = one
        two_ref[...] = two

        def step(n, carry):
            for u in range(ROW_UNROLL):
                i = n * ROW_UNROLL + u
                g = g_ref[s * BS + i]
                at = pl.multiple_of(i * 8, 8)
                for ref, part in ((one_ref, part1), (two_ref, part2)):
                    prod = (g * ref[...]).reshape(BS // 8, 8, 2 * F)
                    part[pl.ds(at, 8), :] = jnp.sum(prod, axis=0)
            return carry

        lax.fori_loop(0, BS // ROW_UNROLL, step, 0)
        t1 = jnp.zeros((BS, 2 * F), jnp.float32)
        t2 = jnp.zeros((BS, 2 * F), jnp.float32)
        for k in range(8):
            t1 = t1 + part1[pl.ds(k, BS, stride=8), :]
            t2 = t2 + part2[pl.ds(k, BS, stride=8), :]
        lane = lax.broadcasted_iota(jnp.int32, (BS, 2 * F), 1)
        gain = jnp.where(lane < F, t1 - pltpu.roll(t1, F, axis=1), pltpu.roll(t2, F, axis=1) + t2)
        add_gain(out_ref, gain, p // 16)
        return carry

    lax.fori_loop(0, SLOTS, slot, 0)


def f32(*shape):
    return pltpu.VMEM(shape, jnp.float32)


VM = pl.BlockSpec(memory_space=pltpu.VMEM)
SM = pl.BlockSpec(memory_space=pltpu.SMEM)


def cost(flops, moved):
    return pl.CostEstimate(flops=flops, bytes_accessed=moved, transcendentals=0)


def gain_col(slot_tile, table, dft, residual, spec):
    far = pl.BlockSpec(memory_space=pl.ANY)
    held = [pltpu.with_memory_space_constraint(x, pltpu.HBM) for x in (slot_tile, table, dft, residual)]
    return pl.pallas_call(
        col_kernel,
        name="col_gain",
        out_shape=(
            jax.ShapeDtypeStruct((16, 16, 2 * F), jnp.bfloat16),
            jax.ShapeDtypeStruct((SLOTS * BS, BS, 2 * F), jnp.float32),
            jax.ShapeDtypeStruct((3 * SLOTS,), jnp.int32),
        ),
        in_specs=[far, far, far, far, VM],
        out_specs=(VM, VM, SM),
        scratch_shapes=[
            pltpu.VMEM((2, CHUNK, BS, L), jnp.bfloat16),
            pltpu.VMEM((2 * L, 4 * F), jnp.bfloat16),
            pltpu.SMEM((SLOTS,), jnp.int32),
            pltpu.SMEM(table.shape, jnp.int32),
            f32(BS, 2 * F),
            f32(BS, 2 * F),
            f32(16, 16, 2 * F),
            pltpu.SemaphoreType.DMA((5,)),
        ],
        compiler_params=pltpu.CompilerParams(vmem_limit_bytes=VMEM_COL),
        cost_estimate=cost(SLOTS * BS * BS * L * 2 * F * 4, residual.size * 2),
    )(*held, spec)


def gain_row(meta, spec, g):
    return pl.pallas_call(
        row_kernel,
        name="row_gain",
        out_shape=jax.ShapeDtypeStruct((16, 16, 2 * F), jnp.float32),
        in_specs=[SM, VM, VM],
        out_specs=VM,
        scratch_shapes=[f32(BS, 2 * F), f32(BS, 2 * F), f32(BS * 8, 2 * F), f32(BS * 8, 2 * F)],
        compiler_params=pltpu.CompilerParams(vmem_limit_bytes=VMEM_ROW),
        cost_estimate=cost(g.size * 4, g.size * 4),
    )(meta, spec, g)


def hops(a, b, k):
    def ring(u, v, n):
        return min((u - v) % n, (v - u) % n)

    z = ring(a // 4 * 2 + b // 8, b // 4 * 2 + k // 8, 8)
    return z + ring(a % 4, b % 4, 4) + ring(b // 2 % 4, k // 2 % 4, 4)


def assign(cost):
    n = len(cost)
    u, v, row, way = [0] * (n + 1), [0] * (n + 1), [0] * (n + 1), [0] * (n + 1)
    for i in range(1, n + 1):
        row[0], at = i, 0
        least, used = [math.inf] * (n + 1), [False] * (n + 1)
        while row[at]:
            used[at] = True
            delta, nxt = math.inf, 0
            for j in range(1, n + 1):
                if not used[j]:
                    c = cost[row[at] - 1][j - 1] - u[row[at]] - v[j]
                    if c < least[j]:
                        least[j], way[j] = c, at
                    if least[j] < delta:
                        delta, nxt = least[j], j
            for j in range(n + 1):
                if used[j]:
                    u[row[j]] += delta
                    v[j] -= delta
                else:
                    least[j] -= delta
            at = nxt
        while at:
            row[at] = row[way[at]]
            at = way[at]
    return {row[j] - 1: j - 1 for j in range(1, n + 1)}


def partners():
    pairs = []
    for b in range(16):
        chosen = assign([[6 ** hops(a, b, k) for k in range(16)] for a in range(16)])
        pairs += [(a * 16 + b, b * 16 + chosen[a]) for a in range(16)]
    return pairs


def on_device(spectra, residual, slot_tile, tile_blocks):
    table = tile_blocks.T
    dft = jnp.asarray(dft_pair())
    pairs = partners()
    spread = jnp.broadcast_to(spectra[None], (16, 16, 2 * F))
    row_spec = lax.all_to_all(spread, "col", 0, 0)
    col_spec = lax.ppermute(row_spec, ("row", "col"), [(v, u) for u, v in pairs])
    col_gain, g, meta = gain_col(slot_tile, table, dft, residual.reshape(SLOTS * BS, BS, L), row_spec)
    moved = lax.ppermute(col_gain, ("row", "col"), pairs)
    row_gain = gain_row(meta, col_spec, g)
    total = (row_gain + moved.astype(jnp.float32)).astype(jnp.bfloat16)
    pieces = lax.all_to_all(total, "col", 0, 0)
    return jnp.sum(pieces.astype(jnp.float32), axis=0)


def solution(mesh):
    return jax.shard_map(
        on_device,
        mesh=mesh,
        in_specs=(
            P(("row", "col"), None),
            P(("row", "col"), None, None, None),
            P(("row", "col")),
            P(),
        ),
        out_specs=P(("row", "col"), None),
        check_vma=False,
    )
```

time: 68 us -> 51.8 us (0.76)
  starting transfers between devices: 17.4 us -> 8.17 us
  blocking collectives: 17.2 us -> 24.3 us
  local copies, waits for them, and re-layouts: 6.83 us -> 0.7 us
  Pallas kernels: 19.6 us -> 15 us
  other arithmetic: 2.26 us -> 0.63 us
  waiting for transfers between devices: 4.2 us -> 2.68 us
    all_to_all x0 -> x1, blocking collectives: none -> 12.8 us  [on_device(): row_spec = lax.all_to_all(spread, 'col', 0, 0)]
    all_to_all x1 -> x0, starting transfers between devices: 7.16 us -> none  [on_device(): row_spec = lax.all_to_all(spread, 'col', 0, 0)]
    all_to_all x1, blocking collectives: 17.2 us -> 11.6 us  [on_device(): pieces = lax.all_to_all(total, 'col', 0, 0)]
    unnamed x8 -> x0, local copies, waits for them, and re-layouts: 5.48 us -> none
    pallas_call x2, Pallas kernels: 19.6 us -> 15 us  [the longest x1 9.48 us: gain_col(): pl.pallas_call(col_kernel, name='col_gain', out_shape=(jax.ShapeDtypeStru...]
    all_to_all x1 -> x0, waiting for transfers between devices: 4.2 us -> none  [on_device(): row_spec = lax.all_to_all(spread, 'col', 0, 0)]
    ppermute x2, waiting for transfers between devices: 0.01 us -> 2.68 us  [the longest x1 2.68 us: on_device(): moved = lax.ppermute(col_gain, ('row', 'col'), pairs)]
    ppermute x2, starting transfers between devices: 10.3 us -> 8.17 us  [the longest x1 8.08 us: on_device(): lax.ppermute(row_spec, ('row', 'col'), [(v, u) for u, v in pairs])]
  transfers between devices with their start and end apart: 3 -> 2, of which waited for: 1 -> 1; matrix products, arithmetic and copies ran while one was open for 2% -> 0% of each run, Pallas kernels for 29% -> 29%
where the time goes in v2:
time: 51.8 us; the launch traced here: 51.5 us
  blocking collectives  24.3 us (47%)
  Pallas kernels  15 us (29%)
  starting transfers between devices  8.17 us (16%)
  waiting for transfers between devices  2.68 us (5%)
  local copies, waits for them, and re-layouts  0.7 us (1%)
  other arithmetic  0.63 us (1%)
    all_to_all x1, blocking collectives, on_device(): row_spec = lax.all_to_all(spread, 'col', 0, 0)  12.8 us
    all_to_all x1, blocking collectives, on_device(): pieces = lax.all_to_all(total, 'col', 0, 0)  11.6 us
    pallas_call x1, Pallas kernels, gain_col(): pl.pallas_call(col_kernel, name='col_gain', out_shape=(jax.ShapeDtypeStru...  9.48 us
    ppermute x1, starting transfers between devices, on_device(): lax.ppermute(row_spec, ('row', 'col'), [(v, u) for u, v in pairs])  8.08 us
    pallas_call x1, Pallas kernels, gain_row(): pl.pallas_call(row_kernel, name='row_gain', out_shape=jax.ShapeDtypeStruc...  5.49 us
    ppermute x1, waiting for transfers between devices, on_device(): moved = lax.ppermute(col_gain, ('row', 'col'), pairs)  2.68 us
  transfers between devices with their start and end apart: 2, of which 1 were waited for; matrix products, arithmetic and copies ran while one was open for 0% of the time, Pallas kernels for 29%

profile of v2, /device:TPU:1, one launch (start us, length us, event | category | flops | bytes accessed | tf_op | source)
XLA Modules:
  0.0 51.5 jit_solution(3711844858866282444)
XLA Ops:
  0.0 0.7 %broadcast_in_dim.2 = bf16[16,16,128]{2,1,0:T(8,128)(2,1)S(1)} broadcast(bf16[16,128]{1,0:T(8,128)(2,1)} %param.5), dimensions={1,2} | broadcast | bytes 69632 | tf_op jit(solution)/shard_map/broadcast_in_dim | solution.py:261
  0.7 12.8 %all_to_all.10.spec_ref = bf16[16,16,128]{2,1,0:T(8,128)(2,1)S(1)} all-to-all(bf16[16,16,128]{2,1,0:T(8,128)(2,1)S(1)} %broadcast_in_dim.2), channel_id=1, replica_groups=mesh['row'=16,'col'=16] {'col'}, dimensions={0} | all-to-all | bytes 131072 | tf_op jit(solution)/shard_map/all_to_all | solution.py:262
  13.5 8.1 %collective-permute-start = (bf16[16,16,128]{2,1,0:T(8,128)(2,1)S(1)}, bf16[16,16,128]{2,1,0:T(8,128)(2,1)S(1)}, u32[]{:S(2)}, u32[]{:S(2)}) collective-permute-start(bf16[16,16,128]{2,1,0:T(8,128)(2,1)S(1)} %all_to_all.10.spec_ref), channel_id=1, source_target_pairs={{4,0},{6,16},{7,32},{5,48},{12,64},{14,80},{15,96},{13,112},{11,12... | collective-permute-start | bytes 196616 | tf_op jit(solution)/shard_map/ppermute | solution.py:263
  21.6 9.5 %col_gain.1 = (bf16[16,16,128]{2,1,0:T(8,128)(2,1)S(1)}, f32[384,128,128]{2,1,0:T(8,128)S(1)}, s32[9]{0:T(128)S(1)}) custom-call(s32[3]{0:T(128)} %slot_hbm.1, s32[2,528]{1,0:T(2,128)} %bitcast.3, bf16[256,256]{1,0:T(8,128)(2,1)} %constant.4.clone.dft_hbm, bf16[384,128,128]{2,1,0:T(8,128)(2,1)} %bitcast.2, bf16[16,16,128]{2,1,0:T(8,128)(2,1)S(1)} %all_to_all.10.spec_ref), custom_call_target="tpu_custom_call" | custom-call | flops 3221225472 | bytes 12582912 | tf_op jit(solution)/shard_map/col_gain/pallas_call | solution.py:174
  31.0 0.1 collective-permute-start.1
  31.1 0.0 collective-permute-done.spec_ref
  31.2 5.5 %row_gain.1 = f32[16,16,128]{2,1,0:T(8,128)S(1)} custom-call(s32[9]{0:T(128)S(1)} %get-tuple-element.8.meta_ref, bf16[16,16,128]{2,1,0:T(8,128)(2,1)S(1)} %collective-permute-done.spec_ref, f32[384,128,128]{2,1,0:T(8,128)S(1)} %get-tuple-element.9.g_ref), custom_call_target="tpu_custom_call" | custom-call | flops 25165824 | bytes 25165824 | tf_op jit(solution)/shard_map/row_gain/pallas_call | solution.py:200
  36.6 2.7 %collective-permute-done.1 = bf16[16,16,128]{2,1,0:T(8,128)(2,1)S(1)} collective-permute-done((bf16[16,16,128]{2,1,0:T(8,128)(2,1)S(1)}, bf16[16,16,128]{2,1,0:T(8,128)(2,1)S(1)}, u32[]{:S(2)}, u32[]{:S(2)}) %collective-permute-start.1) | collective-permute-done | bytes 65568 | tf_op jit(solution)/shard_map/ppermute | solution.py:265
  39.4 11.6 %all_to_all.11 = bf16[16,16,128]{2,1,0:T(8,128)(2,1)S(1)} all-to-all(bf16[16,16,128]{2,1,0:T(8,128)(2,1)S(1)} %add_convert_fusion), channel_id=1, replica_groups=mesh['row'=16,'col'=16] {'col'}, dimensions={0} | all-to-all | bytes 131072 | tf_op jit(solution)/shard_map/all_to_all | solution.py:268
  50.9 0.6 %convert_reduce_fusion = f32[16,128]{1,0:T(8,128)} fusion(bf16[16,16,128]{2,1,0:T(8,128)(2,1)S(1)} %all_to_all.11), kind=kLoop, calls=%fused_computation | loop fusion | flops 63488 | bytes 73728 | tf_op jit(solution)/shard_map/reduce_sum | solution.py:269
  (1 shorter events, 0.0 us)
Async XLA Ops:
  13.5 17.7 %collective-permute-start = (bf16[16,16,128]{2,1,0:T(8,128)(2,1)S(1)}, bf16[16,16,128]{2,1,0:T(8,128)(2,1)S(1)}, u32[]{:S(2)}, u32[]{:S(2)}) collective-permute-start(bf16[16,16,128]{2,1,0:T(8,128)(2,1)S(1)} %all_to_all.10.spec_ref), channel_id=1, source_target_pairs={{4,0},{6,16},{7,32},{5,48},{12,64},{14,80},{15,96},{13,112},{11,12... | collective-permute-start | bytes 196616 | tf_op jit(solution)/shard_map/ppermute | solution.py:263
  31.0 8.3 %collective-permute-start.1 = (bf16[16,16,128]{2,1,0:T(8,128)(2,1)S(1)}, bf16[16,16,128]{2,1,0:T(8,128)(2,1)S(1)}, u32[]{:S(2)}, u32[]{:S(2)}) collective-permute-start(bf16[16,16,128]{2,1,0:T(8,128)(2,1)S(1)} %get-tuple-element.10), channel_id=1, source_target_pairs={{0,4},{16,6},{32,7},{48,5},{64,12},{80,14},{96,15},{112,13},{128,1... | collective-permute-start | bytes 196616 | tf_op jit(solution)/shard_map/ppermute | solution.py:265

commit v3 on v2

--- a/solution.py
+++ b/solution.py
@@ -15,11 +15,11 @@
 BS = 128
 SLOTS = 3
 NB = 32
-CHUNK = 64
+CHUNK = 128
 PARTS = SLOTS * BS // CHUNK
 PER = BS // CHUNK
-ROW_UNROLL = 16
-VMEM_COL = 12 << 20
+ROW_UNROLL = 32
+VMEM_COL = 11 << 20
 VMEM_ROW = 8 << 20
 
 
@@ -55,13 +55,21 @@
 
 
 def mask_chunk(buf, slot, first):
-    def one(n, carry):
-        rows = lax.broadcasted_iota(jnp.int32, (BS, L), 0)
-        keep = jnp.where(rows > first + n, 1.0, 0.0).astype(jnp.bfloat16)
-        buf[slot, n] = buf[slot, n] * keep
+    tile = 16
+
+    def one(r, carry):
+        rows = lax.broadcasted_iota(jnp.int32, (tile, L), 0)
+        keep = jnp.where(rows > r, 1.0, 0.0).astype(jnp.bfloat16)
+        for m in range(CHUNK // tile):
+            below = first + m * tile
+            at = m * tile + r
+            if below:
+                buf[slot, at, :below, :] = jnp.zeros((below, L), jnp.bfloat16)
+            own = slice(below, below + tile)
+            buf[slot, at, own, :] = buf[slot, at, own, :] * keep
         return carry
 
-    lax.fori_loop(0, CHUNK, one, 0)
+    lax.fori_loop(0, tile, one, 0)
 
 
 def col_kernel(
@@ -85,25 +93,30 @@
         meta_ref[SLOTS + s] = table_ref[1, safe]
         meta_ref[2 * SLOTS + s] = jnp.where(tile >= 0, 1, 0)
 
+    for s in range(SLOTS):
+        one, two = spec_pair(spec_ref, meta_ref[s] // 16, meta_ref[2 * SLOTS + s])
+        one_ref[s * BS : (s + 1) * BS, :] = one
+        two_ref[s * BS : (s + 1) * BS, :] = two
+
     def part(h, carry):
         s = h // PER
         first = (h - s * PER) * CHUNK
         slot = lax.rem(h, 2)
-        p, q, filled = meta_ref[s], meta_ref[SLOTS + s], meta_ref[2 * SLOTS + s]
+        p, q = meta_ref[s], meta_ref[SLOTS + s]
 
         @pl.when(h + 1 < PARTS)
         def _():
             chunk_copy(res_hbm, buf, sems, h + 1, 1 - slot).start()
 
-        one, two = spec_pair(spec_ref, p // 16, filled)
-        one_ref[...] = one
-        two_ref[...] = two
         chunk_copy(res_hbm, buf, sems, h, slot).wait()
 
-        @pl.when(p == q)
-        def _():
-            mask_chunk(buf, slot, first)
-
+        for c in range(PER):
+
+            @pl.when((p == q) & (first == c * CHUNK))
+            def _():
+                mask_chunk(buf, slot, c * CHUNK)
+
+        half = q // 16
         t1 = jnp.zeros((BS, 2 * F), jnp.float32)
         t2 = jnp.zeros((BS, 2 * F), jnp.float32)
         for u in range(0, CHUNK, 2):
@@ -112,15 +125,18 @@
             for k in range(2):
                 gk = g[:, k * L : (k + 1) * L]
                 g_ref[h * CHUNK + u + k] = gk
-                t1 = t1 + gk * one_ref[pl.ds(first + u + k, 1), :]
-                t2 = t2 + gk * two_ref[pl.ds(first + u + k, 1), :]
-        lane = lax.broadcasted_iota(jnp.int32, (BS, 2 * F), 1)
+                t1 = t1 + gk * one_ref[pl.ds(h * CHUNK + u + k, 1), :]
+                t2 = t2 + gk * two_ref[pl.ds(h * CHUNK + u + k, 1), :]
+        acc_ref[half, 0] += t1
+        acc_ref[half, 1] += t2
+        return carry
+
+    lax.fori_loop(0, PARTS, part, 0)
+    lane = lax.broadcasted_iota(jnp.int32, (BS, 2 * F), 1)
+    for half in range(2):
+        t1, t2 = acc_ref[half, 0], acc_ref[half, 1]
         gain = jnp.where(lane < F, t1 + pltpu.roll(t1, F, axis=1), pltpu.roll(t2, F, axis=1) - t2)
-        add_gain(acc_ref, gain, q // 16)
-        return carry
-
-    lax.fori_loop(0, PARTS, part, 0)
-    out_ref[...] = acc_ref[...].astype(out_ref.dtype)
+        out_ref[:, half * 8 : (half + 1) * 8, :] = gain.reshape(16, BS // 16, 2 * F).astype(out_ref.dtype)
 
 
 def row_kernel(meta_ref, spec_ref, g_ref, out_ref, one_ref, two_ref, part1, part2):
@@ -186,9 +202,9 @@
             pltpu.VMEM((2 * L, 4 * F), jnp.bfloat16),
             pltpu.SMEM((SLOTS,), jnp.int32),
             pltpu.SMEM(table.shape, jnp.int32),
-            f32(BS, 2 * F),
-            f32(BS, 2 * F),
-            f32(16, 16, 2 * F),
+            f32(SLOTS * BS, 2 * F),
+            f32(SLOTS * BS, 2 * F),
+            f32(2, 2, BS, 2 * F),
             pltpu.SemaphoreType.DMA((5,)),
         ],
         compiler_params=pltpu.CompilerParams(vmem_limit_bytes=VMEM_COL),

time: 51.8 us -> 49.9 us (0.963)
  Pallas kernels: 15 us -> 12.9 us
    pallas_call x1, Pallas kernels: 9.48 us -> 7.62 us  [gain_col(): pl.pallas_call(col_kernel, name='col_gain', out_shape=(jax.ShapeDtypeStru...]
  transfers between devices with their start and end apart: 2 -> 2, of which waited for: 1 -> 1; matrix products, arithmetic and copies ran while one was open for 0% -> 0% of each run, Pallas kernels for 29% -> 26%
where the time goes in v3:
time: 49.9 us; the launch traced here: 49.6 us
  blocking collectives  24.3 us (49%)
  Pallas kernels  12.9 us (26%)
  starting transfers between devices  8.17 us (16%)
  waiting for transfers between devices  2.86 us (6%)
  local copies, waits for them, and re-layouts  0.7 us (1%)
  other arithmetic  0.63 us (1%)
    all_to_all x1, blocking collectives, on_device(): row_spec = lax.all_to_all(spread, 'col', 0, 0)  12.8 us
    all_to_all x1, blocking collectives, on_device(): pieces = lax.all_to_all(total, 'col', 0, 0)  11.5 us
    ppermute x1, starting transfers between devices, on_device(): lax.ppermute(row_spec, ('row', 'col'), [(v, u) for u, v in pairs])  8.08 us
    pallas_call x1, Pallas kernels, gain_col(): pl.pallas_call(col_kernel, name='col_gain', out_shape=(jax.ShapeDtypeStru...  7.62 us
    pallas_call x1, Pallas kernels, gain_row(): pl.pallas_call(row_kernel, name='row_gain', out_shape=jax.ShapeDtypeStruc...  5.31 us
    ppermute x1, waiting for transfers between devices, on_device(): moved = lax.ppermute(col_gain, ('row', 'col'), pairs)  2.86 us
  transfers between devices with their start and end apart: 2, of which 1 were waited for; matrix products, arithmetic and copies ran while one was open for 0% of the time, Pallas kernels for 26%

profile of v3, /device:TPU:1, one launch (start us, length us, event | category | flops | bytes accessed | tf_op | source)
XLA Modules:
  0.0 49.6 jit_solution(15388118734599804102)
XLA Ops:
  0.0 0.7 %broadcast_in_dim.2 = bf16[16,16,128]{2,1,0:T(8,128)(2,1)S(1)} broadcast(bf16[16,128]{1,0:T(8,128)(2,1)} %param.5), dimensions={1,2} | broadcast | bytes 69632 | tf_op jit(solution)/shard_map/broadcast_in_dim | solution.py:277
  0.7 12.8 %all_to_all.10.spec_ref = bf16[16,16,128]{2,1,0:T(8,128)(2,1)S(1)} all-to-all(bf16[16,16,128]{2,1,0:T(8,128)(2,1)S(1)} %broadcast_in_dim.2), channel_id=1, replica_groups=mesh['row'=16,'col'=16] {'col'}, dimensions={0} | all-to-all | bytes 131072 | tf_op jit(solution)/shard_map/all_to_all | solution.py:278
  13.5 8.1 %collective-permute-start = (bf16[16,16,128]{2,1,0:T(8,128)(2,1)S(1)}, bf16[16,16,128]{2,1,0:T(8,128)(2,1)S(1)}, u32[]{:S(2)}, u32[]{:S(2)}) collective-permute-start(bf16[16,16,128]{2,1,0:T(8,128)(2,1)S(1)} %all_to_all.10.spec_ref), channel_id=1, source_target_pairs={{4,0},{6,16},{7,32},{5,48},{12,64},{14,80},{15,96},{13,112},{11,12... | collective-permute-start | bytes 196616 | tf_op jit(solution)/shard_map/ppermute | solution.py:279
  21.6 7.6 %col_gain.1 = (bf16[16,16,128]{2,1,0:T(8,128)(2,1)S(1)}, f32[384,128,128]{2,1,0:T(8,128)S(1)}, s32[9]{0:T(128)S(1)}) custom-call(s32[3]{0:T(128)} %slot_hbm.1, s32[2,528]{1,0:T(2,128)} %bitcast.3, bf16[256,256]{1,0:T(8,128)(2,1)} %constant.4.clone.dft_hbm, bf16[384,128,128]{2,1,0:T(8,128)(2,1)} %bitcast.2, bf16[16,16,128]{2,1,0:T(8,128)(2,1)S(1)} %all_to_all.10.spec_ref), custom_call_target="tpu_custom_call" | custom-call | flops 3221225472 | bytes 12582912 | tf_op jit(solution)/shard_map/col_gain/pallas_call | solution.py:190
  29.2 0.1 collective-permute-start.1
  29.3 0.0 collective-permute-done.spec_ref
  29.3 5.3 %row_gain.1 = f32[16,16,128]{2,1,0:T(8,128)S(1)} custom-call(s32[9]{0:T(128)S(1)} %get-tuple-element.8.meta_ref, bf16[16,16,128]{2,1,0:T(8,128)(2,1)S(1)} %collective-permute-done.spec_ref, f32[384,128,128]{2,1,0:T(8,128)S(1)} %get-tuple-element.9.g_ref), custom_call_target="tpu_custom_call" | custom-call | flops 25165824 | bytes 25165824 | tf_op jit(solution)/shard_map/row_gain/pallas_call | solution.py:216
  34.6 2.9 %collective-permute-done.1 = bf16[16,16,128]{2,1,0:T(8,128)(2,1)S(1)} collective-permute-done((bf16[16,16,128]{2,1,0:T(8,128)(2,1)S(1)}, bf16[16,16,128]{2,1,0:T(8,128)(2,1)S(1)}, u32[]{:S(2)}, u32[]{:S(2)}) %collective-permute-start.1) | collective-permute-done | bytes 65568 | tf_op jit(solution)/shard_map/ppermute | solution.py:281
  37.5 11.5 %all_to_all.11 = bf16[16,16,128]{2,1,0:T(8,128)(2,1)S(1)} all-to-all(bf16[16,16,128]{2,1,0:T(8,128)(2,1)S(1)} %add_convert_fusion), channel_id=1, replica_groups=mesh['row'=16,'col'=16] {'col'}, dimensions={0} | all-to-all | bytes 131072 | tf_op jit(solution)/shard_map/all_to_all | solution.py:284
  49.0 0.6 %convert_reduce_fusion = f32[16,128]{1,0:T(8,128)} fusion(bf16[16,16,128]{2,1,0:T(8,128)(2,1)S(1)} %all_to_all.11), kind=kLoop, calls=%fused_computation | loop fusion | flops 63488 | bytes 73728 | tf_op jit(solution)/shard_map/reduce_sum | solution.py:285
  (1 shorter events, 0.0 us)
Async XLA Ops:
  13.5 15.8 %collective-permute-start = (bf16[16,16,128]{2,1,0:T(8,128)(2,1)S(1)}, bf16[16,16,128]{2,1,0:T(8,128)(2,1)S(1)}, u32[]{:S(2)}, u32[]{:S(2)}) collective-permute-start(bf16[16,16,128]{2,1,0:T(8,128)(2,1)S(1)} %all_to_all.10.spec_ref), channel_id=1, source_target_pairs={{4,0},{6,16},{7,32},{5,48},{12,64},{14,80},{15,96},{13,112},{11,12... | collective-permute-start | bytes 196616 | tf_op jit(solution)/shard_map/ppermute | solution.py:279
  29.2 8.3 %collective-permute-start.1 = (bf16[16,16,128]{2,1,0:T(8,128)(2,1)S(1)}, bf16[16,16,128]{2,1,0:T(8,128)(2,1)S(1)}, u32[]{:S(2)}, u32[]{:S(2)}) collective-permute-start(bf16[16,16,128]{2,1,0:T(8,128)(2,1)S(1)} %get-tuple-element.10), channel_id=1, source_target_pairs={{0,4},{16,6},{32,7},{48,5},{64,12},{80,14},{96,15},{112,13},{128,1... | collective-permute-start | bytes 196616 | tf_op jit(solution)/shard_map/ppermute | solution.py:281

commit v4 on v3

--- a/solution.py
+++ b/solution.py
@@ -19,7 +19,7 @@
 PARTS = SLOTS * BS // CHUNK
 PER = BS // CHUNK
 ROW_UNROLL = 32
-VMEM_COL = 11 << 20
+VMEM_COL = 14 << 20
 VMEM_ROW = 8 << 20
 
 
@@ -77,12 +77,13 @@
     buf, dft_ref, slot_ref, table_ref, one_ref, two_ref, acc_ref, sems,
 ):
     small = [
-        pltpu.make_async_copy(src, dst, sems.at[2 + n])
+        pltpu.make_async_copy(src, dst, sems.at[SLOTS + n])
         for n, (src, dst) in enumerate(((slot_hbm, slot_ref), (table_hbm, table_ref), (dft_hbm, dft_ref)))
     ]
     for copy in small:
         copy.start()
-    chunk_copy(res_hbm, buf, sems, 0, 0).start()
+    for n in range(3):
+        chunk_copy(res_hbm, buf, sems, n, n).start()
     acc_ref[...] = jnp.zeros_like(acc_ref)
     for copy in small:
         copy.wait()
@@ -101,12 +102,8 @@
     def part(h, carry):
         s = h // PER
         first = (h - s * PER) * CHUNK
-        slot = lax.rem(h, 2)
+        slot = h
         p, q = meta_ref[s], meta_ref[SLOTS + s]
-
-        @pl.when(h + 1 < PARTS)
-        def _():
-            chunk_copy(res_hbm, buf, sems, h + 1, 1 - slot).start()
 
         chunk_copy(res_hbm, buf, sems, h, slot).wait()
 
@@ -198,14 +195,14 @@
         in_specs=[far, far, far, far, VM],
         out_specs=(VM, VM, SM),
         scratch_shapes=[
-            pltpu.VMEM((2, CHUNK, BS, L), jnp.bfloat16),
+            pltpu.VMEM((SLOTS, CHUNK, BS, L), jnp.bfloat16),
             pltpu.VMEM((2 * L, 4 * F), jnp.bfloat16),
             pltpu.SMEM((SLOTS,), jnp.int32),
             pltpu.SMEM(table.shape, jnp.int32),
             f32(SLOTS * BS, 2 * F),
             f32(SLOTS * BS, 2 * F),
             f32(2, 2, BS, 2 * F),
-            pltpu.SemaphoreType.DMA((5,)),
+            pltpu.SemaphoreType.DMA((SLOTS + 3,)),
         ],
         compiler_params=pltpu.CompilerParams(vmem_limit_bytes=VMEM_COL),
         cost_estimate=cost(SLOTS * BS * BS * L * 2 * F * 4, residual.size * 2),

time: 49.9 us -> 49.2 us (0.986)
  Pallas kernels: 12.9 us -> 12.3 us
    pallas_call x1, Pallas kernels: 7.62 us -> 6.94 us  [gain_col(): pl.pallas_call(col_kernel, name='col_gain', out_shape=(jax.ShapeDtypeStru...]
  transfers between devices with their start and end apart: 2 -> 2, of which waited for: 1 -> 1; matrix products, arithmetic and copies ran while one was open for 0% -> 0% of each run, Pallas kernels for 26% -> 25%
where the time goes in v4:
time: 49.2 us; the launch traced here: 49 us
  blocking collectives  24.2 us (49%)
  Pallas kernels  12.3 us (25%)
  starting transfers between devices  8.17 us (17%)
  waiting for transfers between devices  3.02 us (6%)
  local copies, waits for them, and re-layouts  0.7 us (1%)
  other arithmetic  0.63 us (1%)
    all_to_all x1, blocking collectives, on_device(): row_spec = lax.all_to_all(spread, 'col', 0, 0)  12.8 us
    all_to_all x1, blocking collectives, on_device(): pieces = lax.all_to_all(total, 'col', 0, 0)  11.4 us
    ppermute x1, starting transfers between devices, on_device(): lax.ppermute(row_spec, ('row', 'col'), [(v, u) for u, v in pairs])  8.08 us
    pallas_call x1, Pallas kernels, gain_col(): pl.pallas_call(col_kernel, name='col_gain', out_shape=(jax.ShapeDtypeStru...  6.94 us
    pallas_call x1, Pallas kernels, gain_row(): pl.pallas_call(row_kernel, name='row_gain', out_shape=jax.ShapeDtypeStruc...  5.31 us
    ppermute x1, waiting for transfers between devices, on_device(): moved = lax.ppermute(col_gain, ('row', 'col'), pairs)  3.02 us
  transfers between devices with their start and end apart: 2, of which 1 were waited for; matrix products, arithmetic and copies ran while one was open for 0% of the time, Pallas kernels for 25%

profile of v4, /device:TPU:1, one launch (start us, length us, event | category | flops | bytes accessed | tf_op | source)
XLA Modules:
  0.0 49.0 jit_solution(6461741372925877971)
XLA Ops:
  0.0 0.7 %broadcast_in_dim.2 = bf16[16,16,128]{2,1,0:T(8,128)(2,1)S(1)} broadcast(bf16[16,128]{1,0:T(8,128)(2,1)} %param.5), dimensions={1,2} | broadcast | bytes 69632 | tf_op jit(solution)/shard_map/broadcast_in_dim | solution.py:274
  0.7 12.8 %all_to_all.10.spec_ref = bf16[16,16,128]{2,1,0:T(8,128)(2,1)S(1)} all-to-all(bf16[16,16,128]{2,1,0:T(8,128)(2,1)S(1)} %broadcast_in_dim.2), channel_id=1, replica_groups=mesh['row'=16,'col'=16] {'col'}, dimensions={0} | all-to-all | bytes 131072 | tf_op jit(solution)/shard_map/all_to_all | solution.py:275
  13.5 8.1 %collective-permute-start = (bf16[16,16,128]{2,1,0:T(8,128)(2,1)S(1)}, bf16[16,16,128]{2,1,0:T(8,128)(2,1)S(1)}, u32[]{:S(2)}, u32[]{:S(2)}) collective-permute-start(bf16[16,16,128]{2,1,0:T(8,128)(2,1)S(1)} %all_to_all.10.spec_ref), channel_id=1, source_target_pairs={{4,0},{6,16},{7,32},{5,48},{12,64},{14,80},{15,96},{13,112},{11,12... | collective-permute-start | bytes 196616 | tf_op jit(solution)/shard_map/ppermute | solution.py:276
  21.6 6.9 %col_gain.1 = (bf16[16,16,128]{2,1,0:T(8,128)(2,1)S(1)}, f32[384,128,128]{2,1,0:T(8,128)S(1)}, s32[9]{0:T(128)S(1)}) custom-call(s32[3]{0:T(128)} %slot_hbm.1, s32[2,528]{1,0:T(2,128)} %bitcast.3, bf16[256,256]{1,0:T(8,128)(2,1)} %constant.4.clone.dft_hbm, bf16[384,128,128]{2,1,0:T(8,128)(2,1)} %bitcast.2, bf16[16,16,128]{2,1,0:T(8,128)(2,1)S(1)} %all_to_all.10.spec_ref), custom_call_target="tpu_custom_call" | custom-call | flops 3221225472 | bytes 12582912 | tf_op jit(solution)/shard_map/col_gain/pallas_call | solution.py:187
  28.5 0.1 collective-permute-start.1
  28.6 0.0 collective-permute-done.spec_ref
  28.6 5.3 %row_gain.1 = f32[16,16,128]{2,1,0:T(8,128)S(1)} custom-call(s32[9]{0:T(128)S(1)} %get-tuple-element.8.meta_ref, bf16[16,16,128]{2,1,0:T(8,128)(2,1)S(1)} %collective-permute-done.spec_ref, f32[384,128,128]{2,1,0:T(8,128)S(1)} %get-tuple-element.9.g_ref), custom_call_target="tpu_custom_call" | custom-call | flops 25165824 | bytes 25165824 | tf_op jit(solution)/shard_map/row_gain/pallas_call | solution.py:213
  33.9 3.0 %collective-permute-done.1 = bf16[16,16,128]{2,1,0:T(8,128)(2,1)S(1)} collective-permute-done((bf16[16,16,128]{2,1,0:T(8,128)(2,1)S(1)}, bf16[16,16,128]{2,1,0:T(8,128)(2,1)S(1)}, u32[]{:S(2)}, u32[]{:S(2)}) %collective-permute-start.1) | collective-permute-done | bytes 65568 | tf_op jit(solution)/shard_map/ppermute | solution.py:278
  37.0 11.4 %all_to_all.11 = bf16[16,16,128]{2,1,0:T(8,128)(2,1)S(1)} all-to-all(bf16[16,16,128]{2,1,0:T(8,128)(2,1)S(1)} %add_convert_fusion), channel_id=1, replica_groups=mesh['row'=16,'col'=16] {'col'}, dimensions={0} | all-to-all | bytes 131072 | tf_op jit(solution)/shard_map/all_to_all | solution.py:281
  48.4 0.6 %convert_reduce_fusion = f32[16,128]{1,0:T(8,128)} fusion(bf16[16,16,128]{2,1,0:T(8,128)(2,1)S(1)} %all_to_all.11), kind=kLoop, calls=%fused_computation | loop fusion | flops 63488 | bytes 73728 | tf_op jit(solution)/shard_map/reduce_sum | solution.py:282
  (1 shorter events, 0.0 us)
Async XLA Ops:
  13.5 15.1 %collective-permute-start = (bf16[16,16,128]{2,1,0:T(8,128)(2,1)S(1)}, bf16[16,16,128]{2,1,0:T(8,128)(2,1)S(1)}, u32[]{:S(2)}, u32[]{:S(2)}) collective-permute-start(bf16[16,16,128]{2,1,0:T(8,128)(2,1)S(1)} %all_to_all.10.spec_ref), channel_id=1, source_target_pairs={{4,0},{6,16},{7,32},{5,48},{12,64},{14,80},{15,96},{13,112},{11,12... | collective-permute-start | bytes 196616 | tf_op jit(solution)/shard_map/ppermute | solution.py:276
  28.5 8.5 %collective-permute-start.1 = (bf16[16,16,128]{2,1,0:T(8,128)(2,1)S(1)}, bf16[16,16,128]{2,1,0:T(8,128)(2,1)S(1)}, u32[]{:S(2)}, u32[]{:S(2)}) collective-permute-start(bf16[16,16,128]{2,1,0:T(8,128)(2,1)S(1)} %get-tuple-element.10), channel_id=1, source_target_pairs={{0,4},{16,6},{32,7},{48,5},{64,12},{80,14},{96,15},{112,13},{128,1... | collective-permute-start | bytes 196616 | tf_op jit(solution)/shard_map/ppermute | solution.py:278

commit v5 on v4

--- a/solution.py
+++ b/solution.py
@@ -15,10 +15,10 @@
 BS = 128
 SLOTS = 3
 NB = 32
-CHUNK = 128
+CHUNK = 64
 PARTS = SLOTS * BS // CHUNK
 PER = BS // CHUNK
-ROW_UNROLL = 32
+ROW_UNROLL = 64
 VMEM_COL = 14 << 20
 VMEM_ROW = 8 << 20
 
@@ -77,12 +77,12 @@
     buf, dft_ref, slot_ref, table_ref, one_ref, two_ref, acc_ref, sems,
 ):
     small = [
-        pltpu.make_async_copy(src, dst, sems.at[SLOTS + n])
+        pltpu.make_async_copy(src, dst, sems.at[PARTS + n])
         for n, (src, dst) in enumerate(((slot_hbm, slot_ref), (table_hbm, table_ref), (dft_hbm, dft_ref)))
     ]
     for copy in small:
         copy.start()
-    for n in range(3):
+    for n in range(PARTS):
         chunk_copy(res_hbm, buf, sems, n, n).start()
     acc_ref[...] = jnp.zeros_like(acc_ref)
     for copy in small:
@@ -195,14 +195,14 @@
         in_specs=[far, far, far, far, VM],
         out_specs=(VM, VM, SM),
         scratch_shapes=[
-            pltpu.VMEM((SLOTS, CHUNK, BS, L), jnp.bfloat16),
+            pltpu.VMEM((PARTS, CHUNK, BS, L), jnp.bfloat16),
             pltpu.VMEM((2 * L, 4 * F), jnp.bfloat16),
             pltpu.SMEM((SLOTS,), jnp.int32),
             pltpu.SMEM(table.shape, jnp.int32),
             f32(SLOTS * BS, 2 * F),
             f32(SLOTS * BS, 2 * F),
             f32(2, 2, BS, 2 * F),
-            pltpu.SemaphoreType.DMA((SLOTS + 3,)),
+            pltpu.SemaphoreType.DMA((PARTS + 3,)),
         ],
         compiler_params=pltpu.CompilerParams(vmem_limit_bytes=VMEM_COL),
         cost_estimate=cost(SLOTS * BS * BS * L * 2 * F * 4, residual.size * 2),

time: 49.2 us -> 49.1 us (level)
  no operation moved by 1% of the time
where the time goes in v5:
time: 49.1 us; the launch traced here: 48.9 us
  blocking collectives  24.3 us (49%)
  Pallas kernels  12.1 us (25%)
  starting transfers between devices  8.17 us (17%)
  waiting for transfers between devices  2.94 us (6%)
  local copies, waits for them, and re-layouts  0.7 us (1%)
  other arithmetic  0.63 us (1%)
    all_to_all x1, blocking collectives, on_device(): row_spec = lax.all_to_all(spread, 'col', 0, 0)  12.8 us
    all_to_all x1, blocking collectives, on_device(): pieces = lax.all_to_all(total, 'col', 0, 0)  11.5 us
    ppermute x1, starting transfers between devices, on_device(): lax.ppermute(row_spec, ('row', 'col'), [(v, u) for u, v in pairs])  8.08 us
    pallas_call x1, Pallas kernels, gain_col(): pl.pallas_call(col_kernel, name='col_gain', out_shape=(jax.ShapeDtypeStru...  6.92 us
    pallas_call x1, Pallas kernels, gain_row(): pl.pallas_call(row_kernel, name='row_gain', out_shape=jax.ShapeDtypeStruc...  5.23 us
    ppermute x1, waiting for transfers between devices, on_device(): moved = lax.ppermute(col_gain, ('row', 'col'), pairs)  2.94 us
  transfers between devices with their start and end apart: 2, of which 1 were waited for; matrix products, arithmetic and copies ran while one was open for 0% of the time, Pallas kernels for 25%

profile of v5, /device:TPU:1, one launch (start us, length us, event | category | flops | bytes accessed | tf_op | source)
XLA Modules:
  0.0 48.9 jit_solution(18121936014903265917)
XLA Ops:
  0.0 0.7 %broadcast_in_dim.2 = bf16[16,16,128]{2,1,0:T(8,128)(2,1)S(1)} broadcast(bf16[16,128]{1,0:T(8,128)(2,1)} %param.5), dimensions={1,2} | broadcast | bytes 69632 | tf_op jit(solution)/shard_map/broadcast_in_dim | solution.py:274
  0.7 12.8 %all_to_all.10.spec_ref = bf16[16,16,128]{2,1,0:T(8,128)(2,1)S(1)} all-to-all(bf16[16,16,128]{2,1,0:T(8,128)(2,1)S(1)} %broadcast_in_dim.2), channel_id=1, replica_groups=mesh['row'=16,'col'=16] {'col'}, dimensions={0} | all-to-all | bytes 131072 | tf_op jit(solution)/shard_map/all_to_all | solution.py:275
  13.5 8.1 %collective-permute-start = (bf16[16,16,128]{2,1,0:T(8,128)(2,1)S(1)}, bf16[16,16,128]{2,1,0:T(8,128)(2,1)S(1)}, u32[]{:S(2)}, u32[]{:S(2)}) collective-permute-start(bf16[16,16,128]{2,1,0:T(8,128)(2,1)S(1)} %all_to_all.10.spec_ref), channel_id=1, source_target_pairs={{4,0},{6,16},{7,32},{5,48},{12,64},{14,80},{15,96},{13,112},{11,12... | collective-permute-start | bytes 196616 | tf_op jit(solution)/shard_map/ppermute | solution.py:276
  21.6 6.9 %col_gain.1 = (bf16[16,16,128]{2,1,0:T(8,128)(2,1)S(1)}, f32[384,128,128]{2,1,0:T(8,128)S(1)}, s32[9]{0:T(128)S(1)}) custom-call(s32[3]{0:T(128)} %slot_hbm.1, s32[2,528]{1,0:T(2,128)} %bitcast.3, bf16[256,256]{1,0:T(8,128)(2,1)} %constant.4.clone.dft_hbm, bf16[384,128,128]{2,1,0:T(8,128)(2,1)} %bitcast.2, bf16[16,16,128]{2,1,0:T(8,128)(2,1)S(1)} %all_to_all.10.spec_ref), custom_call_target="tpu_custom_call" | custom-call | flops 3221225472 | bytes 12582912 | tf_op jit(solution)/shard_map/col_gain/pallas_call | solution.py:187
  28.5 0.1 collective-permute-start.1
  28.6 0.0 collective-permute-done.spec_ref
  28.6 5.2 %row_gain.1 = f32[16,16,128]{2,1,0:T(8,128)S(1)} custom-call(s32[9]{0:T(128)S(1)} %get-tuple-element.8.meta_ref, bf16[16,16,128]{2,1,0:T(8,128)(2,1)S(1)} %collective-permute-done.spec_ref, f32[384,128,128]{2,1,0:T(8,128)S(1)} %get-tuple-element.9.g_ref), custom_call_target="tpu_custom_call" | custom-call | flops 25165824 | bytes 25165824 | tf_op jit(solution)/shard_map/row_gain/pallas_call | solution.py:213
  33.8 2.9 %collective-permute-done.1 = bf16[16,16,128]{2,1,0:T(8,128)(2,1)S(1)} collective-permute-done((bf16[16,16,128]{2,1,0:T(8,128)(2,1)S(1)}, bf16[16,16,128]{2,1,0:T(8,128)(2,1)S(1)}, u32[]{:S(2)}, u32[]{:S(2)}) %collective-permute-start.1) | collective-permute-done | bytes 65568 | tf_op jit(solution)/shard_map/ppermute | solution.py:278
  36.8 11.5 %all_to_all.11 = bf16[16,16,128]{2,1,0:T(8,128)(2,1)S(1)} all-to-all(bf16[16,16,128]{2,1,0:T(8,128)(2,1)S(1)} %add_convert_fusion), channel_id=1, replica_groups=mesh['row'=16,'col'=16] {'col'}, dimensions={0} | all-to-all | bytes 131072 | tf_op jit(solution)/shard_map/all_to_all | solution.py:281
  48.3 0.6 %convert_reduce_fusion = f32[16,128]{1,0:T(8,128)} fusion(bf16[16,16,128]{2,1,0:T(8,128)(2,1)S(1)} %all_to_all.11), kind=kLoop, calls=%fused_computation | loop fusion | flops 63488 | bytes 73728 | tf_op jit(solution)/shard_map/reduce_sum | solution.py:282
  (1 shorter events, 0.0 us)
Async XLA Ops:
  13.5 15.1 %collective-permute-start = (bf16[16,16,128]{2,1,0:T(8,128)(2,1)S(1)}, bf16[16,16,128]{2,1,0:T(8,128)(2,1)S(1)}, u32[]{:S(2)}, u32[]{:S(2)}) collective-permute-start(bf16[16,16,128]{2,1,0:T(8,128)(2,1)S(1)} %all_to_all.10.spec_ref), channel_id=1, source_target_pairs={{4,0},{6,16},{7,32},{5,48},{12,64},{14,80},{15,96},{13,112},{11,12... | collective-permute-start | bytes 196616 | tf_op jit(solution)/shard_map/ppermute | solution.py:276
  28.5 8.3 %collective-permute-start.1 = (bf16[16,16,128]{2,1,0:T(8,128)(2,1)S(1)}, bf16[16,16,128]{2,1,0:T(8,128)(2,1)S(1)}, u32[]{:S(2)}, u32[]{:S(2)}) collective-permute-start(bf16[16,16,128]{2,1,0:T(8,128)(2,1)S(1)} %get-tuple-element.10), channel_id=1, source_target_pairs={{0,4},{16,6},{32,7},{48,5},{64,12},{80,14},{96,15},{112,13},{128,1... | collective-permute-start | bytes 196616 | tf_op jit(solution)/shard_map/ppermute | solution.py:278
